TPU v7x, 32 devices: a whole 2x2x4 slice. The times are simulated.
32 devices in a mesh: fsdp: 4 (over y, core), ctx: 8 (over z, x).
Axes of the slice: x: 2, y: 2, z: 4, core: 2. Of those that a mesh axis runs over, the one named last changes fastest.
Arguments:
- inputs: bfloat16 [4, 4096, 1536], P('fsdp', 'ctx'), may hold values from -8 to 8
- segment_ids: int32 [4, 4096], P('fsdp', 'ctx'), may hold values from 0 to 3, never falling along the last dimension, each value on 1 to 2048 neighbouring positions
- out_grad: bfloat16 [4, 4096, 1536], P('fsdp', 'ctx'), may hold values from -6 to 6
- in_matrix: bfloat16 [1536, 6448], P('fsdp'), may hold values from -0.15625 to 0.15625
- out_matrix: bfloat16 [3072, 1536], P('fsdp'), may hold values from -0.109375 to 0.109375
- conv_taps: bfloat16 [3328, 4], P('fsdp'), may hold values from -3 to 3
- conv_bias: bfloat16 [3328], P('fsdp'), may hold values from -2.5 to 2.5
- dt_bias: bfloat16 [48], P('fsdp'), may hold values from -6 to -2
- decay_log: bfloat16 [48], P('fsdp'), may hold values from -7 to 2.5
- skip_scale: bfloat16 [48], P('fsdp'), may hold values from 0.5 to 2
- mixer_gain: bfloat16 [3072], P('fsdp'), may hold values from 0.5 to 1.5
- input_gain: bfloat16 [1536], P('fsdp'), may hold values from 0.5 to 1.5
Outputs:
- block_out: bfloat16 [4, 4096, 1536], P('fsdp', 'ctx')
- input_grad: bfloat16 [4, 4096, 1536], P('fsdp', 'ctx')
- in_matrix_grad: float32 [1536, 6448], P('fsdp')
- out_matrix_grad: float32 [3072, 1536], P('fsdp')
- conv_taps_grad: float32 [3328, 4], P('fsdp')
- conv_bias_grad: float32 [3328], P('fsdp')
- dt_bias_grad: float32 [48], P('fsdp')
- decay_log_grad: float32 [48], P('fsdp')
- skip_scale_grad: float32 [48], P('fsdp')
- mixer_gain_grad: float32 [3072], P('fsdp')
- input_gain_grad: float32 [1536], P('fsdp')
- rms_stats: float32 [2], replicated
Inputs may be any that keep to these rules, and one draw needn't show every extreme that they name: `segment_ids`: along each sequence the numbers never fall; a run of equal numbers is one document; every number of 0 to 3 is used, and the longest document has exactly 2048 tokens.
All inputs are finite; a program needn't handle non-finite values.
Results may differ from a plain program's by a relative error of at most 0.015.
Values may be sent and summed in bfloat16 or wider, within the bound.
A program may use at most 320 MiB of HBM per device.

v0:
```python
import jax
import jax.numpy as jnp
from jax import lax
from jax.sharding import PartitionSpec as P

D = 1536
HEADS = 48
HDIM = 64
STATE = 128
CONV = 4
GROUP = 256
INNER = 3072
XBC = 3328
epsilon = 1e-05
precise = lax.Precision.HIGHEST


def passed_along(block, axis, distance):
    devices = range(lax.axis_size(axis))
    route = [(i - distance, i) for i in devices if i - distance in devices]
    return lax.ppermute(block, axis, route)


def prefix(x, axis, join, neutral):
    place = lax.axis_index(axis)
    gathered = jax.tree.map(
        lambda a, kind: lax.all_gather(a.astype(kind), axis), x, (jnp.bfloat16, jnp.bfloat16)
    )
    state = jax.tree.map(lambda a, e: jnp.zeros_like(a) + jnp.asarray(e, a.dtype), x, neutral)

    def one(lap, state):
        return join(
            state,
            jax.tree.map(
                lambda a, own: lax.dynamic_index_in_dim(a, lap, 0, False).astype(own.dtype),
                gathered,
                x,
            ),
        )

    return lax.fori_loop(0, place, one, state)


def prefix_2(x, axis, combine, identity):
    count, mine = (lax.axis_size(axis), lax.axis_index(axis))
    everything = jax.tree.map(
        lambda part, kind: lax.all_gather(part.astype(kind), axis),
        x,
        jax.tree.map(lambda a: jnp.bfloat16 if a.dtype == jnp.float32 else a.dtype, x),
    )
    start = jax.tree.map(
        lambda part, zero: jnp.broadcast_to(jnp.asarray(zero, part.dtype), part.shape), x, identity
    )

    def lap(k, before):
        at = count - 1 - k
        reached = at > mine
        new = combine(
            before, jax.tree.map(lambda part, own: part[at].astype(own.dtype), everything, x)
        )
        return jax.tree.map(lambda a, b: jnp.where(reached, a, b), new, before)

    return lax.fori_loop(0, count, lap, start)


def combine(earlier, later_pair):
    return (earlier[0] * later_pair[0], later_pair[0][:, None, None] * earlier[1] + later_pair[1])


def block_step(carry_pair, sliced):
    carried, seg_before, offset = carry_pair
    xblock, bblock, cblock, dblock, lblock, sblock = sliced
    block_len = sblock.shape[0]
    running = jnp.cumsum(lblock, axis=0)
    rowpos = lax.broadcasted_iota(jnp.int32, (block_len, block_len), 0)
    colpos = lax.broadcasted_iota(jnp.int32, (block_len, block_len), 1)
    allowed = (sblock[:, None] == sblock[None, :]) & (colpos <= rowpos)
    log_gap = running.T[:, :, None] - running.T[:, None, :]
    decays = jnp.exp(jnp.where(allowed[None], log_gap, -1e30))
    scores = jnp.dot(cblock, bblock.T, precision=precise)
    mixing = decays * scores[None] * dblock.T[:, None, :]
    y_diag = jnp.einsum("hts,shp->thp", mixing, xblock, precision=precise)
    carry_in = (sblock == seg_before).astype(jnp.float32)
    y_off = (jnp.exp(running) * carry_in[:, None])[:, :, None] * jnp.einsum(
        "tn,hpn->thp", cblock, carried, precision=precise
    )
    final_log = running[block_len - 1]
    tail_weight = (
        jnp.exp(final_log[None, :] - running)
        * (sblock == sblock[block_len - 1]).astype(jnp.float32)[:, None]
        * dblock
    )
    retain = jnp.exp(final_log) * (sblock[block_len - 1] == seg_before).astype(jnp.float32)
    carried = retain[:, None, None] * carried + jnp.einsum(
        "sh,shp,sn->hpn", tail_weight, xblock, bblock, precision=precise
    )
    return (
        (carried, sblock[block_len - 1], offset + final_log),
        (y_diag + y_off, running + offset[None, :]),
    )


def scan_ssd(values, b_rows, c_rows, dt_rows, log_decay, seg_ids, seg_start):
    length = seg_ids.shape[0]
    blocks = length // GROUP
    sliced = (
        values.reshape(blocks, GROUP, HEADS, HDIM),
        b_rows.reshape(blocks, GROUP, STATE),
        c_rows.reshape(blocks, GROUP, STATE),
        dt_rows.reshape(blocks, GROUP, HEADS),
        log_decay.reshape(blocks, GROUP, HEADS),
        seg_ids.reshape(blocks, GROUP),
    )
    initial = (
        jnp.zeros((HEADS, HDIM, STATE), jnp.float32),
        seg_start,
        jnp.zeros((HEADS,), jnp.float32),
    )
    finish, (outputs, running) = lax.scan(jax.checkpoint(block_step), initial, sliced)
    return (outputs.reshape(length, HEADS, HDIM), running.reshape(length, HEADS), finish[0])


def mixer_front(
    ext_rows, dt_raw, conv_taps, conv_bias, dt_bias, decay_log, seg_ext, seg_ids, seg_start
):
    length = seg_ids.shape[0]
    summed = jnp.broadcast_to(conv_bias, (length, conv_bias.shape[0]))
    for tap_index in range(CONV):
        same_doc = (seg_ext[tap_index : tap_index + length] == seg_ids).astype(jnp.float32)
        summed = (
            summed
            + conv_taps[:, tap_index] * ext_rows[tap_index : tap_index + length] * same_doc[:, None]
        )
    active = jax.nn.silu(summed)
    values = active[:, :INNER].reshape(length, HEADS, HDIM)
    b_rows = active[:, INNER : INNER + STATE]
    c_rows = active[:, INNER + STATE :]
    dt_rows = jax.nn.softplus(dt_raw + dt_bias)
    log_decay = -dt_rows * jnp.exp(decay_log)
    y_local, running, carried = scan_ssd(
        values, b_rows, c_rows, dt_rows, log_decay, seg_ids, seg_start
    )
    retain = jnp.exp(running[length - 1]) * (seg_ids[length - 1] == seg_start).astype(jnp.float32)
    return (values, c_rows, running, y_local, carried, retain)


def mixer_tail(
    values, c_rows, running, y_local, carried_in, gate_part, skip_scale, mixer_gain, carry_flag
):
    length = gate_part.shape[0]
    incoming = jnp.einsum("tn,hpn->thp", c_rows, carried_in, precision=precise)
    weights = jnp.exp(running) * carry_flag[:, None]
    mixed_ssd = y_local + weights[:, :, None] * incoming + skip_scale[None, :, None] * values
    gated = mixed_ssd.reshape(length, INNER) * jax.nn.silu(gate_part)
    return gated * lax.rsqrt(jnp.mean(gated * gated, axis=-1, keepdims=True) + epsilon) * mixer_gain


def on_device(
    inputs,
    segment_ids,
    out_grad,
    in_matrix,
    out_matrix,
    conv_taps,
    conv_bias,
    dt_bias,
    decay_log,
    skip_scale,
    mixer_gain,
    input_gain,
):
    units = inputs[0].astype(jnp.float32)
    seg_ids = segment_ids[0]
    length = units.shape[0]
    inv_rms = lax.rsqrt(jnp.mean(units * units, axis=-1, keepdims=True) + epsilon)
    base_rows = units * inv_rms
    w_piece = lax.all_gather(in_matrix, "fsdp", axis=0, tiled=True)
    g_piece = lax.all_gather(input_gain, "fsdp", axis=0, tiled=True)
    g_float = g_piece.astype(jnp.float32)
    part_rows = (base_rows * g_float).astype(jnp.bfloat16)
    product = jnp.dot(part_rows, w_piece, preferred_element_type=jnp.float32)
    projected = product
    projected = projected.astype(jnp.bfloat16)
    gate_part = projected[:, :INNER].astype(jnp.float32)
    conv_input = projected[:, INNER : INNER + XBC]
    dt_raw = projected[:, INNER + XBC :].astype(jnp.float32)
    out_whole, taps_whole, bias_whole, dtb_whole, decay_whole, skip_whole, norm_whole = (
        lax.all_gather(out_matrix, "fsdp", axis=0, tiled=True),
        lax.all_gather(conv_taps, "fsdp", axis=0, tiled=True),
        lax.all_gather(conv_bias, "fsdp", axis=0, tiled=True),
        lax.all_gather(dt_bias, "fsdp", axis=0, tiled=True),
        lax.all_gather(decay_log, "fsdp", axis=0, tiled=True),
        lax.all_gather(skip_scale, "fsdp", axis=0, tiled=True),
        lax.all_gather(mixer_gain, "fsdp", axis=0, tiled=True),
    )
    rim_rows, rim_seg = passed_along(
        (conv_input[length - CONV + 1 :], seg_ids[length - CONV + 1 :]), "ctx", 1
    )
    ext_rows = jnp.concatenate([rim_rows, conv_input], axis=0).astype(jnp.float32)
    seg_ext = jnp.concatenate([rim_seg, seg_ids], axis=0)
    seg_start = rim_seg[CONV - 2]

    def front_fn(ext_arg, dt_arg, taps_arg, bias_arg, dtb_arg, decay_arg):
        return mixer_front(
            ext_arg, dt_arg, taps_arg, bias_arg, dtb_arg, decay_arg, seg_ext, seg_ids, seg_start
        )

    front_out, front_back = jax.vjp(
        front_fn,
        ext_rows,
        dt_raw,
        taps_whole.astype(jnp.float32),
        bias_whole.astype(jnp.float32),
        dtb_whole.astype(jnp.float32),
        decay_whole.astype(jnp.float32),
    )
    values, c_rows, running, y_local, carried, retain = front_out
    identity = (jnp.ones((HEADS,), jnp.float32), jnp.zeros((HEADS, HDIM, STATE), jnp.float32))
    passed = prefix((retain, carried), "ctx", combine, identity)
    carried_in = passed[1]
    carry_flag = (seg_ids == seg_start).astype(jnp.float32)

    def tail_fn(
        values_arg, c_arg, running_arg, local_arg, carried_arg, gate_arg, skip_arg, gain_arg
    ):
        return mixer_tail(
            values_arg,
            c_arg,
            running_arg,
            local_arg,
            carried_arg,
            gate_arg,
            skip_arg,
            gain_arg,
            carry_flag,
        )

    mixer_out, tail_back = jax.vjp(
        tail_fn,
        values,
        c_rows,
        running,
        y_local,
        carried_in,
        gate_part,
        skip_whole.astype(jnp.float32),
        norm_whole.astype(jnp.float32),
    )
    mixer_low = mixer_out.astype(jnp.bfloat16)
    mixed = jnp.dot(mixer_low, out_whole, preferred_element_type=jnp.float32)
    summed_out = units + mixed
    block_out = summed_out.astype(jnp.bfloat16)
    cot_rows = out_grad[0]
    d_out_matrix = lax.dot_general(
        mixer_low, cot_rows, (((0,), (0,)), ((), ())), preferred_element_type=jnp.float32
    )
    d_mixer = lax.dot_general(
        cot_rows, out_whole, (((1,), (1,)), ((), ())), preferred_element_type=jnp.float32
    )
    d_values, d_c_rows, d_running, d_local, d_carried, d_gate, d_skip, d_norm_gain = tail_back(
        d_mixer
    )
    reversed_pair = prefix_2((retain, d_carried), "ctx", combine, identity)
    d_state = reversed_pair[1]
    d_retain = jnp.sum(d_state * carried_in, axis=(1, 2))
    d_ext, d_dt_raw, d_taps, d_bias, d_dtb, d_decay = front_back(
        (d_values, d_c_rows, d_running, d_local, d_state, d_retain)
    )
    returned = passed_along(d_ext[: CONV - 1].astype(jnp.bfloat16), "ctx", -1).astype(jnp.float32)
    d_conv_in = jnp.concatenate([d_ext[CONV - 1 : length], d_ext[length:] + returned], axis=0)
    d_projected = jnp.concatenate([d_gate, d_conv_in, d_dt_raw], axis=1).astype(jnp.bfloat16)
    d_in_matrix = lax.dot_general(
        part_rows, d_projected, (((0,), (0,)), ((), ())), preferred_element_type=jnp.float32
    )
    d_normed = lax.dot_general(
        d_projected,
        lax.all_gather(in_matrix, "fsdp", axis=0, tiled=True),
        (((1,), (1,)), ((), ())),
        preferred_element_type=jnp.float32,
    )
    d_input_gain = jnp.sum(d_normed * base_rows, axis=0)
    d_base = d_normed * g_float
    d_units = inv_rms * (d_base - base_rows * jnp.mean(d_base * base_rows, axis=-1, keepdims=True))
    input_grad = (cot_rows.astype(jnp.float32) + d_units).astype(jnp.bfloat16)
    split_sums = (
        lax.psum_scatter(
            d_in_matrix.astype(jnp.bfloat16), "fsdp", scatter_dimension=0, tiled=True
        ).astype(jnp.float32),
        lax.psum_scatter(
            d_out_matrix.astype(jnp.bfloat16), "fsdp", scatter_dimension=0, tiled=True
        ).astype(jnp.float32),
        lax.psum_scatter(
            d_taps.astype(jnp.bfloat16), "fsdp", scatter_dimension=0, tiled=True
        ).astype(jnp.float32),
        lax.psum_scatter(
            d_bias.astype(jnp.bfloat16), "fsdp", scatter_dimension=0, tiled=True
        ).astype(jnp.float32),
        lax.psum_scatter(
            d_norm_gain.astype(jnp.bfloat16), "fsdp", scatter_dimension=0, tiled=True
        ).astype(jnp.float32),
        lax.psum_scatter(
            d_input_gain.astype(jnp.bfloat16), "fsdp", scatter_dimension=0, tiled=True
        ).astype(jnp.float32),
    )
    reduced = (
        lax.psum(split_sums[0].astype(jnp.bfloat16), "ctx").astype(jnp.float32),
        lax.psum(split_sums[1].astype(jnp.bfloat16), "ctx").astype(jnp.float32),
        lax.psum(split_sums[2].astype(jnp.bfloat16), "ctx").astype(jnp.float32),
        lax.psum(split_sums[3].astype(jnp.bfloat16), "ctx").astype(jnp.float32),
        lax.psum(split_sums[4].astype(jnp.bfloat16), "ctx").astype(jnp.float32),
        lax.psum(split_sums[5].astype(jnp.bfloat16), "ctx").astype(jnp.float32),
    )
    square_sums = jnp.stack([jnp.sum(summed_out * summed_out), jnp.sum(mixed * mixed)])
    head_dt, head_decay, head_skip, stat_sums = lax.psum(
        (d_dtb, d_decay, d_skip, square_sums), ("fsdp", "ctx")
    )
    per_shard = HEADS // lax.axis_size("fsdp")
    offset_rows = lax.axis_index("fsdp") * per_shard
    dt_grad = lax.dynamic_slice_in_dim(head_dt, offset_rows, per_shard, 0)
    decay_grad = lax.dynamic_slice_in_dim(head_decay, offset_rows, per_shard, 0)
    skip_grad = lax.dynamic_slice_in_dim(head_skip, offset_rows, per_shard, 0)
    entries = length * lax.axis_size("fsdp") * lax.axis_size("ctx") * D
    rms_stats = jnp.sqrt(stat_sums / entries)
    return (
        block_out[None],
        input_grad[None],
        reduced[0],
        reduced[1],
        reduced[2],
        reduced[3],
        dt_grad,
        decay_grad,
        skip_grad,
        reduced[4],
        reduced[5],
        rms_stats,
    )


def solution(mesh):
    return jax.shard_map(
        on_device,
        mesh=mesh,
        in_specs=(
            P("fsdp", "ctx", None),
            P("fsdp", "ctx"),
            P("fsdp", "ctx", None),
            P("fsdp", None),
            P("fsdp", None),
            P("fsdp", None),
            P("fsdp"),
            P("fsdp"),
            P("fsdp"),
            P("fsdp"),
            P("fsdp"),
            P("fsdp"),
        ),
        out_specs=(
            P("fsdp", "ctx", None),
            P("fsdp", "ctx", None),
            P("fsdp", None),
            P("fsdp", None),
            P("fsdp", None),
            P("fsdp"),
            P("fsdp"),
            P("fsdp"),
            P("fsdp"),
            P("fsdp"),
            P("fsdp"),
            P(),
        ),
        check_vma=False,
    )
```

profile of v0, /device:TPU:0, one launch (start us, length us, event | category | flops | bytes accessed | tf_op | source)
XLA Modules:
  0.0 1636.9 jit_solution(982712403689798339)
XLA Ops:
  25.6 8.2 all-reduce.24
  33.8 5.5 all-gather.3
  44.6 93.2 %all-gather.11.cloned.1.call-done = bf16[1536,6448]{0,1:T(8,128)(2,1)} async-done(((bf16[384,6448]{0,1:T(8,128)(2,1)}), bf16[1536,6448]{0,1:T(8,128)(2,1)}) %all-gather.11.cloned.1.call-update) | async-done | bytes 19808272 | tf_op jit(solution)/shard_map/all_gather | solution.py:177
  137.8 16.7 %convolution_convert_fusion.2 = bf16[512,6448]{1,0:T(8,128)(2,1)} fusion(bf16[1536,6448]{0,1:T(8,128)(2,1)} %all-gather.11.cloned.1.call-done, bf16[1,512,1536]{2,1,0:T(8,128)(2,1)S(1)} %copy-done.14, f32[1536]{0:T(1024)S(1)} %reshape.551, f32[512]{0:T(512)S(1)} %add_rsqrt_fusion), kind=kOutput, calls=%fused_computation.150 | convolution fusion | flops 10148274176 | bytes 27992064 | tf_op jit(solution)/shard_map/dot_general | solution.py:181
  167.6 8.4 fusion.93
  175.9 6.1 slice.212
  183.9 6.6 copy.271
  190.5 8.2 reshape.509
  198.7 6.3 copy.274
  205.0 210.1 %while.80 = (s32[]{:T(128)}, f32[48,64,128]{2,1,0:T(8,128)S(1)}, s32[]{:T(128)}, f32[48]{0:T(128)S(1)}, f32[2,256,48,64]{1,0,3,2:T(2,128)}, /*index=5*/f32[2,256...) while((s32[]{:T(128)}, f32[48,64,128]{2,1,0:T(8,128)S(1)}, ...), condition=%wide.region_4.5_spmd.clone, body=%wide.region_1.4_spmd.clone.sunk | while | flops 4951254016 | bytes 38503760 | solution.py:119
  208.6 16.5 %fusion.240 = f32[48,64,256]{2,1,0:T(8,128)} fusion(f32[48,256]{1,0:T(8,128)S(1)} %dynamic-slice_bitcast_fusion.17, f32[256,256]{1,0:T(8,128)S(1)} %fusion.238, f32[48,256]{1,0:T(8,128)S(1)} %get-tuple-element.1556, pred[256,256]{1,0:T(8,128)(4,1)S(1)} %fusion.239, f32[2,256,48,64]{1,3,2,0:T(8,128)} %get-tuple-element.1663, s32[]{:T(128)} %get-tuple-element.1634), kind=kOutput, calls=%fused_computation.6.clone.1 | convolution fusion | flops 2428502016 | bytes 6767104 | tf_op jit(solution)/shard_map/jvp()/while/body/eval_jaxpr/hts,shp->thp/dot_general | solution.py:82
  236.9 63.6 %dynamic_update_slice.95 = f32[2,256,48,64]{1,0,3,2:T(2,128)} dynamic-update-slice(f32[2,256,48,64]{1,0,3,2:T(2,128)} %get-tuple-element.1638, f32[1,256,48,64]{1,0,3,2:T(1,128)} %copy.397, s32[]{:T(128)} %get-tuple-element.1634, s32[]{:T(128)} %constant.198.clone.1..sunk.1, s32[]{:T(128)} %constant.198.clone.1..sunk.1, s32[]{:T(128)} %constant.198.clone.1..sunk.1) | dynamic-update-slice | bytes 6291460 | tf_op jit(solution)/shard_map/jvp()/while/body/jit(dynamic_update_index_in_dim)/dynamic_update_slice | solution.py:119
  313.4 16.5 %fusion.240 = f32[48,64,256]{2,1,0:T(8,128)} fusion(f32[48,256]{1,0:T(8,128)S(1)} %dynamic-slice_bitcast_fusion.17, f32[256,256]{1,0:T(8,128)S(1)} %fusion.238, f32[48,256]{1,0:T(8,128)S(1)} %get-tuple-element.1556, pred[256,256]{1,0:T(8,128)(4,1)S(1)} %fusion.239, f32[2,256,48,64]{1,3,2,0:T(8,128)} %get-tuple-element.1663, s32[]{:T(128)} %get-tuple-element.1634), kind=kOutput, calls=%fused_computation.6.clone.1 | convolution fusion | flops 2428502016 | bytes 6767104 | tf_op jit(solution)/shard_map/jvp()/while/body/eval_jaxpr/hts,shp->thp/dot_general | solution.py:82
  341.7 63.6 %dynamic_update_slice.95 = f32[2,256,48,64]{1,0,3,2:T(2,128)} dynamic-update-slice(f32[2,256,48,64]{1,0,3,2:T(2,128)} %get-tuple-element.1638, f32[1,256,48,64]{1,0,3,2:T(1,128)} %copy.397, s32[]{:T(128)} %get-tuple-element.1634, s32[]{:T(128)} %constant.198.clone.1..sunk.1, s32[]{:T(128)} %constant.198.clone.1..sunk.1, s32[]{:T(128)} %constant.198.clone.1..sunk.1) | dynamic-update-slice | bytes 6291460 | tf_op jit(solution)/shard_map/jvp()/while/body/jit(dynamic_update_index_in_dim)/dynamic_update_slice | solution.py:119
  417.6 5.2 all-gather.5
  425.2 18.4 %all-gather.4 = bf16[8,1,48]{2,1,0:T(2,128)(2,1)S(1)} all-gather(bf16[1,1,48]{2,1,0:T(2,128)(2,1)S(1)} %bitcast.512), channel_id=1, replica_groups=mesh['fsdp'=4,'ctx'=8] {'ctx'}, dimensions={0}, use_global_device_ids=true | all-gather | bytes 864 | tf_op jit(solution)/shard_map/all_gather | solution.py:27
  443.6 9.0 reshape.512
  452.6 61.9 %all-gather.15.cloned.1.call-done = bf16[384,64,128]{2,1,0:T(8,128)(2,1)} async-done(((bf16[48,64,128]{2,1,0:T(8,128)(2,1)}), bf16[384,64,128]{2,1,0:T(8,128)(2,1)}) %all-gather.15.cloned.1.call-update) | async-done | bytes 6291472 | tf_op jit(solution)/shard_map/all_gather | solution.py:27
  514.7 13.1 multiply_add_fusion.4
  527.8 6.6 copy.278
  534.4 6.8 multiply_reduce_fusion.13
  541.2 37.4 %all-gather.13.cloned.1.call-done = bf16[3072,1536]{1,0:T(8,128)(2,1)} async-done(((bf16[768,1536]{1,0:T(8,128)(2,1)}), bf16[3072,1536]{1,0:T(8,128)(2,1)}) %all-gather.13.cloned.1.call-update) | async-done | bytes 9437200 | tf_op jit(solution)/shard_map/all_gather | solution.py:188
  578.6 12.5 multiply_reduce_fusion.9
  591.1 11.2 multiply_reduce_fusion.10
  602.3 6.5 copy.280
  608.8 8.2 fusion.126
  617.9 10.2 reshape.581
  628.0 11.0 copy.286
  639.0 6.4 multiply_reduce_fusion.11
  645.4 70.8 %all-gather.17.cloned.1.call-done = bf16[384,64,128]{2,1,0:T(8,128)(2,1)} async-done(((bf16[48,64,128]{2,1,0:T(8,128)(2,1)}), bf16[384,64,128]{2,1,0:T(8,128)(2,1)}) %all-gather.17.cloned.1.call-update) | async-done | bytes 6291472 | tf_op jit(solution)/shard_map/all_gather | solution.py:47
  716.2 24.0 %while.81 = (s32[]{:T(128)}, f32[48,64,128]{2,1,0:T(8,128)}, s32[]{:T(128)}, bf16[8,48]{1,0:T(8,128)(2,1)S(1)}, bf16[8,48,64,128]{3,2,1,0:T(8,128)(2,1)}, /*index=5*/s32[]{:T(128)}, s32[]{:T(128)}, s32[]{:T(128)}, s32[]{:T(128)}) while((s32[]{:T(128)}, f32[48,64,128]{2,1,0:T(8,128)}, s32[]{:T(128)}, ...), condition=%wide.region_10.11_spmd.clone, body=%wide.region_9.10_spmd.clone.sunk | while | flops 1966136 | bytes 3932807 | solution.py:63
  749.2 248.0 %while.82 = (s32[]{:T(128)}, f32[48,64,128]{2,1,0:T(8,128)}, f32[48]{0:T(128)}, f32[2,256,48,64]{1,3,2,0:T(8,128)}, f32[2,256,128]{2,1,0:T(8,128)}, /*index=5*/f...) while((s32[]{:T(128)}, f32[48,64,128]{2,1,0:T(8,128)}, ...), condition=%wide.region_26.27_spmd.clone, body=%wide.region_13.26_spmd.clone.sunk | while | flops 11239392256 | bytes 115198616 | solution.py:119
  769.1 5.3 dynamic-slice_bitcast_fusion.19
  785.5 6.7 multiply_reduce_fusion.21
  809.2 21.4 %fusion.264 = (f32[48,256]{1,0:T(8,128)S(1)}, f32[48,256]{1,0:T(8,128)S(1)}, f32[48,256]{1,0:T(8,128)}, f32[256,256]{1,0:T(8,128)}) fusion(f32[48,256]{1,0:T(8,128)S(1)} %bitcast.484, f32[256,256]{1,0:T(8,128)S(1)} %fusion.262, f32[48,256]{1,0:T(8,128)} %get-tuple-element.1594, pred[256,256]{1,0:T(8,128)(4,1)S(1)} %fusion.263, ...), kind=kOutput, calls=%fused_computation.72.clone.1 | convolution fusion | flops 2456711168 | bytes 7127040 | tf_op jit(solution)/shard_map/transpose(jvp())/while/body/eval_jaxpr/checkpoint/hts,shp->thp/dot_general | solution.py:82
  844.3 6.4 fusion.269
  852.8 6.5 fusion.267
  860.7 12.2 bitcast_dynamic-update-slice_fusion.7
  878.7 5.3 dynamic-slice_bitcast_fusion.19
  895.7 6.7 multiply_reduce_fusion.21
  919.4 21.4 %fusion.264 = (f32[48,256]{1,0:T(8,128)S(1)}, f32[48,256]{1,0:T(8,128)S(1)}, f32[48,256]{1,0:T(8,128)}, f32[256,256]{1,0:T(8,128)}) fusion(f32[48,256]{1,0:T(8,128)S(1)} %bitcast.484, f32[256,256]{1,0:T(8,128)S(1)} %fusion.262, f32[48,256]{1,0:T(8,128)} %get-tuple-element.1594, pred[256,256]{1,0:T(8,128)(4,1)S(1)} %fusion.263, ...), kind=kOutput, calls=%fused_computation.72.clone.1 | convolution fusion | flops 2456711168 | bytes 7127040 | tf_op jit(solution)/shard_map/transpose(jvp())/while/body/eval_jaxpr/checkpoint/hts,shp->thp/dot_general | solution.py:82
  954.6 6.4 fusion.269
  963.0 6.5 fusion.267
  971.0 12.2 bitcast_dynamic-update-slice_fusion.7
  997.2 12.7 fusion.132
  1009.9 11.3 copy.299
  1021.2 10.8 reshape.582
  1032.0 6.0 multiply_add_fusion.3
  1038.1 10.7 multiply_reduce_fusion.8
  1048.8 8.2 broadcast_multiply_fusion
  1057.0 8.0 fusion.165
  1075.3 16.4 convolution_convert_fusion
  1091.6 24.2 %copy.300 = bf16[1536,6448]{1,0:T(8,128)(2,1)} copy(bf16[1536,6448]{0,1:T(8,128)(2,1)} %convolution_convert_fusion) | data formatting | bytes 39616512
  1117.2 11.2 convolution_convert_fusion.1
  1130.3 133.6 %reduce-scatter.10.cloned.1.call-done = bf16[384,6448]{1,0:T(8,128)(2,1)} async-done(((bf16[1536,6448]{1,0:T(8,128)(2,1)}), bf16[384,6448]{1,0:T(8,128)(2,1)}) %reduce-scatter.10.cloned.1.call-update) | async-done | bytes 4952080
  1264.0 7.6 copy.301
  1271.5 74.1 %reduce-scatter.8.cloned.1.call-done = bf16[768,1536]{1,0:T(8,128)(2,1)} async-done(((bf16[3072,1536]{1,0:T(8,128)(2,1)}), bf16[768,1536]{1,0:T(8,128)(2,1)}) %reduce-scatter.8.cloned.1.call-update) | async-done | bytes 2359312 | tf_op jit(solution)/shard_map/reduce_scatter | solution.py:289
  1348.0 20.0 %fusion.135 = f32[512,1536]{1,0:T(8,128)S(1)} fusion(bf16[1536,6448]{0,1:T(8,128)(2,1)} %all-gather.11.cloned.1.call-done, bf16[512,48]{1,0:T(8,128)(2,1)S(1)} %copy-done.49, bf16[3,3328]{1,0:T(4,128)(2,1)S(1)} %fusion.147, bf16[509,3328]{1,0:T(8,128)(2,1)} %copy-done.19, bf16[512,3072]{1,0:T(8,128)(2,1)} %get-tuple-element.1248), kind=kOutput, calls=%fused_computation.222 | convolution fusion | flops 10168238080 | bytes 29556736 | tf_op jit(solution)/shard_map/dot_general | solution.py:275
  1368.1 12.7 multiply_reduce_fusion.15
  1382.2 44.0 %all-reduce.20 = (f32[48]{0:T(128)S(1)}, f32[48]{0:T(128)S(1)}, f32[48]{0:T(128)S(1)}, f32[2]{0:T(128)S(1)}) all-reduce(f32[48]{0:T(128)S(1)} %copy-done.80, f32[48]{0:T(128)S(1)} %fusion.156, f32[48]{0:T(128)S(1)} %reduce_sum.376, f32[2]{0:T(128)S(1)} %pad_maximum_fusion.3), channel_id=1, replica_groups=mesh['fsdp'=4,'ctx'=8] {'fsdp','ctx'}, use_global_device_ids=true, to_apply=%region_42.43 | all-reduce | flops 146 | bytes 1168 | tf_op jit(solution)/shard_map/psum | solution.py:314
  1427.9 11.9 all-reduce.23
  1446.5 37.0 %all-reduce.21 = (bf16[832,4]{0,1:T(4,128)(2,1)S(1)}, bf16[832]{0:T(1024)(128)(2,1)S(1)}, bf16[768]{0:T(1024)(128)(2,1)S(1)}, bf16[384]{0:T(512)(128)(2,1)S(1)}) all-reduce(bf16[832,4]{0,1:T(4,128)(2,1)S(1)} %copy.303, bf16[832]{0:T(1024)(128)(2,1)S(1)} %dynamic-slice.5, ...), channel_id=1, replica_groups=mesh['fsdp'=4,'ctx'=8] {'ctx'}, use_global_device_ids=true, to_apply=%region_37.38 | all-reduce | flops 5312 | bytes 21248 | tf_op jit(solution)/shard_map/psum | solution.py:308
  1485.9 133.8 %all-reduce.27.cloned.1.call-done = (bf16[384,6448]{0,1:T(8,128)(2,1)}, bf16[768,1536]{1,0:T(8,128)(2,1)}) async-done(((bf16[384,6448]{0,1:T(8,128)(2,1)}, bf16[768,1536]{1,0:T(8,128)(2,1)}), (bf16[384,6448]{0,1:T(8,128)(2,1)}, bf16[768,1536]{1,0:T(8,128)(2,1)})) %all-reduce.27.cloned.1.call-update) | async-done | bytes 7311376 | tf_op jit(solution)/shard_map/psum | solution.py:306
  1619.7 7.1 convert_element_type.263
  (495 shorter events, 248.6 us)
Async XLA Ops:
  7.2 36.1 %copy-start.68 = (s32[1,512]{1,0:T(1,128)S(1)}, s32[1,512]{1,0:T(1,128)}, u32[]{:S(2)}) copy-start(s32[1,512]{1,0:T(1,128)} %param.21) | copy-start | bytes 6148
  7.2 34.3 %copy-start.14 = (bf16[1,512,1536]{2,1,0:T(8,128)(2,1)S(1)}, bf16[1,512,1536]{2,1,0:T(8,128)(2,1)}, u32[]{:S(2)}) copy-start(bf16[1,512,1536]{2,1,0:T(8,128)(2,1)} %param.20) | copy-start | bytes 4718596
  7.2 130.6 %all-gather.11.cloned.1.call-start = ((), (), s32[]{:S(2)}) async-start(), calls=%async_computation.3 | async-start | bytes 24760320 | tf_op jit(solution)/shard_map/all_gather | solution.py:177
  7.9 506.6 %all-gather.15.cloned.1.call-start = ((), (), s32[]{:S(2)}) async-start(), calls=%async_computation.6 | async-start | bytes 7077888 | tf_op jit(solution)/shard_map/all_gather | solution.py:27
  8.7 33.3 %collective-permute-start = (s32[3]{0:T(128)S(1)}, s32[3]{0:T(128)S(1)}, u32[]{:S(2)}, u32[]{:S(2)}) collective-permute-start(s32[3]{0:T(128)S(1)} %slice_bitcast_fusion), channel_id=1, source_target_pairs={{0,1},{1,2},{2,3},{3,4},{4,5},{5,6},{6,7},{8,9},{9,10},{10,11},{11... | collective-permute-start | bytes 44 | tf_op jit(solution)/shard_map/ppermute | solution.py:21
  19.5 135.0 %copy-start.65 = (f32[1536]{0:T(1024)}, f32[1536]{0:T(1024)S(1)}, u32[]{:S(2)}) copy-start(f32[1536]{0:T(1024)S(1)} %reshape.551) | copy-start | bytes 18436
  33.8 120.7 %copy-start.83 = (bf16[48]{0:T(256)(128)(2,1)}, bf16[48]{0:T(256)(128)(2,1)S(1)}, u32[]{:S(2)}) copy-start(bf16[48]{0:T(256)(128)(2,1)S(1)} %get-tuple-element.1206) | copy-start | bytes 292
  39.5 119.4 %copy-start.76 = (f32[48]{0:T(128)}, f32[48]{0:T(128)S(1)}, u32[]{:S(2)}) copy-start(f32[48]{0:T(128)S(1)} %convert_element_type.241) | copy-start | bytes 580
  41.5 126.0 %copy-start.40 = (f32[3328]{0:T(1024)}, f32[3328]{0:T(1024)S(1)}, u32[]{:S(2)}) copy-start(f32[3328]{0:T(1024)S(1)} %get-tuple-element.1104) | copy-start | bytes 39940
  41.5 126.0 %copy-start.42 = (f32[3328]{0:T(1024)}, f32[3328]{0:T(1024)S(1)}, u32[]{:S(2)}) copy-start(f32[3328]{0:T(1024)S(1)} %get-tuple-element.1105) | copy-start | bytes 39940
  41.6 126.0 %copy-start.44 = (f32[3328]{0:T(1024)}, f32[3328]{0:T(1024)S(1)}, u32[]{:S(2)}) copy-start(f32[3328]{0:T(1024)S(1)} %get-tuple-element.1106) | copy-start | bytes 39940
  41.6 126.0 %copy-start.46 = (f32[3328]{0:T(1024)}, f32[3328]{0:T(1024)S(1)}, u32[]{:S(2)}) copy-start(f32[3328]{0:T(1024)S(1)} %get-tuple-element.1107) | copy-start | bytes 39940
  42.0 117.0 %copy-start.78 = (f32[48]{0:T(128)}, f32[48]{0:T(128)S(1)}, u32[]{:S(2)}) copy-start(f32[48]{0:T(128)S(1)} %convert_exponential_fusion) | copy-start | bytes 580
  42.0 112.5 %copy-start.73 = (f32[512]{0:T(512)}, f32[512]{0:T(512)S(1)}, u32[]{:S(2)}) copy-start(f32[512]{0:T(512)S(1)} %add_rsqrt_fusion) | copy-start | bytes 6148
  44.6 123.0 %copy-start.59 = (f32[512]{0:T(512)}, f32[512]{0:T(512)S(1)}, u32[]{:S(2)}) copy-start(f32[512]{0:T(512)S(1)} %get-tuple-element.1259) | copy-start | bytes 6148
  44.6 123.0 %copy-start.61 = (f32[512]{0:T(512)}, f32[512]{0:T(512)S(1)}, u32[]{:S(2)}) copy-start(f32[512]{0:T(512)S(1)} %get-tuple-element.1260) | copy-start | bytes 6148
  44.6 123.0 %copy-start.63 = (f32[512]{0:T(512)}, f32[512]{0:T(512)S(1)}, u32[]{:S(2)}) copy-start(f32[512]{0:T(512)S(1)} %get-tuple-element.1261) | copy-start | bytes 6148
  155.3 9.5 collective-permute-start.1
  205.0 212.5 %copy-start.81 = (bf16[768]{0:T(1024)(128)(2,1)S(1)}, bf16[768]{0:T(1024)(128)(2,1)}, u32[]{:S(2)}) copy-start(bf16[768]{0:T(1024)(128)(2,1)} %param.30) | copy-start | bytes 4612
  415.1 37.5 %copy-start.50 = (s32[2,256]{1,0:T(2,128)}, s32[2,256]{1,0:T(2,128)S(1)}, u32[]{:S(2)}) copy-start(s32[2,256]{1,0:T(2,128)S(1)} %get-tuple-element.1822) | copy-start | bytes 6148
  416.2 162.4 %all-gather.13.cloned.1.call-start = ((), (), s32[]{:S(2)}) async-start(), calls=%async_computation.4 | async-start | bytes 11796480 | tf_op jit(solution)/shard_map/all_gather | solution.py:188
  416.9 299.3 %all-gather.17.cloned.1.call-start = ((), (), s32[]{:S(2)}) async-start(), calls=%async_computation.7 | async-start | bytes 7077888 | tf_op jit(solution)/shard_map/all_gather | solution.py:47
  422.7 168.4 %copy-start.55 = (f32[4,1,768]{2,1,0:T(1,128)}, f32[4,1,768]{2,1,0:T(1,128)S(1)}, u32[]{:S(2)}) copy-start(f32[4,1,768]{2,1,0:T(1,128)S(1)} %convert_element_type.281) | copy-start | bytes 36868
  452.6 156.2 %copy-start.24 = (f32[512,48]{0,1:T(8,128)}, f32[512,48]{0,1:T(8,128)S(1)}, u32[]{:S(2)}) copy-start(f32[512,48]{0,1:T(8,128)S(1)} %exponential_multiply_fusion.4) | copy-start | bytes 294916
  514.7 225.5 %copy-start.2 = (f32[48,64,128]{2,1,0:T(8,128)}, f32[48,64,128]{2,1,0:T(8,128)S(1)}, u32[]{:S(2)}) copy-start(f32[48,64,128]{2,1,0:T(8,128)S(1)} %get-tuple-element.688) | copy-start | bytes 4718596
  534.4 44.2 %copy-start.27 = (bf16[1,512,1536]{2,1,0:T(8,128)(2,1)S(1)}, bf16[1,512,1536]{2,1,0:T(8,128)(2,1)}, u32[]{:S(2)}) copy-start(bf16[1,512,1536]{2,1,0:T(8,128)(2,1)} %param.22) | copy-start | bytes 4718596
  541.2 49.9 %copy-start.71 = (f32[512]{0:T(512)}, f32[512]{0:T(512)S(1)}, u32[]{:S(2)}) copy-start(f32[512]{0:T(512)S(1)} %fusion.153) | copy-start | bytes 6148
  617.1 646.9 %reduce-scatter.10.cloned.1.call-start = ((), (), s32[]{:S(2)}) async-start(), calls=%async_computation.8 | async-start | bytes 25067520
  776.8 32.3 %copy-start.8 = (f32[256,48]{0,1:T(8,128)}, f32[256,48]{0,1:T(8,128)S(1)}, u32[]{:S(2)}) copy-start(f32[256,48]{0,1:T(8,128)S(1)} %get-tuple-element.1590) | copy-start | bytes 147460 | tf_op jit(solution)/shard_map/transpose(jvp())/while
  808.3 22.4 %copy-start.12 = (f32[256,256]{1,0:T(8,128)}, f32[256,256]{1,0:T(8,128)S(1)}, u32[]{:S(2)}) copy-start(f32[256,256]{1,0:T(8,128)S(1)} %fusion.262) | copy-start | bytes 786436 | tf_op jit(solution)/shard_map/transpose(jvp())/while
  809.1 21.5 %copy-start.25 = (pred[256,256]{1,0:T(8,128)(4,1)}, pred[256,256]{1,0:T(8,128)(4,1)S(1)}, u32[]{:S(2)}) copy-start(pred[256,256]{1,0:T(8,128)(4,1)S(1)} %fusion.263) | copy-start | bytes 196612 | tf_op jit(solution)/shard_map/transpose(jvp())/while
  809.1 21.5 %copy-start.18 = (f32[1,256,48]{1,2,0:T(8,128)S(1)}, f32[1,256,48]{1,2,0:T(8,128)}, u32[]{:S(2)}) copy-start(f32[1,256,48]{1,2,0:T(8,128)} %copy.405) | copy-start | bytes 147460 | tf_op jit(solution)/shard_map/transpose(jvp())/while
  809.2 21.5 %copy-start.22 = (f32[1,48]{0,1:T(8,128)S(1)}, f32[1,48]{0,1:T(8,128)}, u32[]{:S(2)}) copy-start(f32[1,48]{0,1:T(8,128)} %copy.406) | copy-start | bytes 580 | tf_op jit(solution)/shard_map/transpose(jvp())/while
  809.2 21.5 %copy-start.35 = (f32[48,2]{0,1:T(2,128)S(1)}, f32[48,2]{0,1:T(2,128)}, u32[]{:S(2)}) copy-start(f32[48,2]{0,1:T(2,128)} %copy-done.34) | copy-start | bytes 1156 | tf_op jit(solution)/shard_map/transpose(jvp())/while
  809.2 21.5 %copy-start.36 = (f32[256]{0:T(256)S(1)}, f32[256]{0:T(256)}, u32[]{:S(2)}) copy-start(f32[256]{0:T(256)} %get-tuple-element.1602) | copy-start | bytes 3076 | tf_op jit(solution)/shard_map/transpose(jvp())/while
  809.2 21.5 %copy-start.39 = (f32[48]{0:T(128)S(1)}, f32[48]{0:T(128)}, u32[]{:S(2)}) copy-start(f32[48]{0:T(128)} %copy-done.38) | copy-start | bytes 580 | tf_op jit(solution)/shard_map/transpose(jvp())/while
  809.2 21.5 %copy-start.52 = (f32[256]{0:T(256)S(1)}, f32[256]{0:T(256)}, u32[]{:S(2)}) copy-start(f32[256]{0:T(256)} %get-tuple-element.1607) | copy-start | bytes 3076 | tf_op jit(solution)/shard_map/transpose(jvp())/while
  840.0 20.6 %copy-start.3 = (f32[256,48,64]{0,2,1:T(8,128)S(1)}, f32[256,48,64]{0,2,1:T(8,128)}, u32[]{:S(2)}) copy-start(f32[256,48,64]{0,2,1:T(8,128)} %get-tuple-element.1611) | copy-start | bytes 9437188 | tf_op jit(solution)/shard_map/transpose(jvp())/while
  840.0 20.6 %copy-start.9 = (f32[256,48]{0,1:T(8,128)S(1)}, f32[256,48]{0,1:T(8,128)}, u32[]{:S(2)}) copy-start(f32[256,48]{0,1:T(8,128)} %copy-done.8) | copy-start | bytes 147460 | tf_op jit(solution)/shard_map/transpose(jvp())/while
  840.0 20.6 %copy-start.13 = (f32[256,256]{1,0:T(8,128)S(1)}, f32[256,256]{1,0:T(8,128)}, u32[]{:S(2)}) copy-start(f32[256,256]{1,0:T(8,128)} %copy-done.12) | copy-start | bytes 786436 | tf_op jit(solution)/shard_map/transpose(jvp())/while
  886.4 33.0 %copy-start.8 = (f32[256,48]{0,1:T(8,128)}, f32[256,48]{0,1:T(8,128)S(1)}, u32[]{:S(2)}) copy-start(f32[256,48]{0,1:T(8,128)S(1)} %get-tuple-element.1590) | copy-start | bytes 147460 | tf_op jit(solution)/shard_map/transpose(jvp())/while
  918.5 22.4 %copy-start.12 = (f32[256,256]{1,0:T(8,128)}, f32[256,256]{1,0:T(8,128)S(1)}, u32[]{:S(2)}) copy-start(f32[256,256]{1,0:T(8,128)S(1)} %fusion.262) | copy-start | bytes 786436 | tf_op jit(solution)/shard_map/transpose(jvp())/while
  919.4 21.5 %copy-start.25 = (pred[256,256]{1,0:T(8,128)(4,1)}, pred[256,256]{1,0:T(8,128)(4,1)S(1)}, u32[]{:S(2)}) copy-start(pred[256,256]{1,0:T(8,128)(4,1)S(1)} %fusion.263) | copy-start | bytes 196612 | tf_op jit(solution)/shard_map/transpose(jvp())/while
  919.4 21.5 %copy-start.18 = (f32[1,256,48]{1,2,0:T(8,128)S(1)}, f32[1,256,48]{1,2,0:T(8,128)}, u32[]{:S(2)}) copy-start(f32[1,256,48]{1,2,0:T(8,128)} %copy.405) | copy-start | bytes 147460 | tf_op jit(solution)/shard_map/transpose(jvp())/while
  919.4 21.5 %copy-start.22 = (f32[1,48]{0,1:T(8,128)S(1)}, f32[1,48]{0,1:T(8,128)}, u32[]{:S(2)}) copy-start(f32[1,48]{0,1:T(8,128)} %copy.406) | copy-start | bytes 580 | tf_op jit(solution)/shard_map/transpose(jvp())/while
  919.4 21.5 %copy-start.35 = (f32[48,2]{0,1:T(2,128)S(1)}, f32[48,2]{0,1:T(2,128)}, u32[]{:S(2)}) copy-start(f32[48,2]{0,1:T(2,128)} %copy-done.34) | copy-start | bytes 1156 | tf_op jit(solution)/shard_map/transpose(jvp())/while
  919.4 21.5 %copy-start.36 = (f32[256]{0:T(256)S(1)}, f32[256]{0:T(256)}, u32[]{:S(2)}) copy-start(f32[256]{0:T(256)} %get-tuple-element.1602) | copy-start | bytes 3076 | tf_op jit(solution)/shard_map/transpose(jvp())/while
  919.4 21.5 %copy-start.39 = (f32[48]{0:T(128)S(1)}, f32[48]{0:T(128)}, u32[]{:S(2)}) copy-start(f32[48]{0:T(128)} %copy-done.38) | copy-start | bytes 580 | tf_op jit(solution)/shard_map/transpose(jvp())/while
  919.4 21.5 %copy-start.52 = (f32[256]{0:T(256)S(1)}, f32[256]{0:T(256)}, u32[]{:S(2)}) copy-start(f32[256]{0:T(256)} %get-tuple-element.1607) | copy-start | bytes 3076 | tf_op jit(solution)/shard_map/transpose(jvp())/while
  950.3 20.7 %copy-start.3 = (f32[256,48,64]{0,2,1:T(8,128)S(1)}, f32[256,48,64]{0,2,1:T(8,128)}, u32[]{:S(2)}) copy-start(f32[256,48,64]{0,2,1:T(8,128)} %get-tuple-element.1611) | copy-start | bytes 9437188 | tf_op jit(solution)/shard_map/transpose(jvp())/while
  950.3 20.7 %copy-start.9 = (f32[256,48]{0,1:T(8,128)S(1)}, f32[256,48]{0,1:T(8,128)}, u32[]{:S(2)}) copy-start(f32[256,48]{0,1:T(8,128)} %copy-done.8) | copy-start | bytes 147460 | tf_op jit(solution)/shard_map/transpose(jvp())/while
  950.3 20.6 %copy-start.13 = (f32[256,256]{1,0:T(8,128)S(1)}, f32[256,256]{1,0:T(8,128)}, u32[]{:S(2)}) copy-start(f32[256,256]{1,0:T(8,128)} %copy-done.12) | copy-start | bytes 786436 | tf_op jit(solution)/shard_map/transpose(jvp())/while
  950.3 20.6 %copy-start.17 = (f32[256,48]{0,1:T(8,128)S(1)}, f32[256,48]{0,1:T(8,128)}, u32[]{:S(2)}) copy-start(f32[256,48]{0,1:T(8,128)} %get-tuple-element.1612) | copy-start | bytes 147460 | tf_op jit(solution)/shard_map/transpose(jvp())/while
  950.3 20.6 %copy-start.26 = (pred[256,256]{1,0:T(8,128)(4,1)S(1)}, pred[256,256]{1,0:T(8,128)(4,1)}, u32[]{:S(2)}) copy-start(pred[256,256]{1,0:T(8,128)(4,1)} %copy-done.25) | copy-start | bytes 196612 | tf_op jit(solution)/shard_map/transpose(jvp())/while
  1065.7 7.9 collective-permute-start.2
  1115.9 229.8 %reduce-scatter.8.cloned.1.call-start = ((), (), s32[]{:S(2)}) async-start(), calls=%async_computation.5 | async-start | bytes 11796480 | tf_op jit(solution)/shard_map/reduce_scatter | solution.py:289
  1128.5 317.0 %reduce-scatter.12.cloned.1.call-start = ((), (), s32[]{:S(2)}) async-start(), calls=%async_computation.9 | async-start | bytes 1064960
  1130.0 217.8 %copy-start.57 = (f32[3072]{0:T(1024)S(1)}, f32[3072]{0:T(1024)}, u32[]{:S(2)}) copy-start(f32[3072]{0:T(1024)} %get-tuple-element.1211) | copy-start | bytes 36868
  1130.0 218.0 %copy-start.82 = (f32[48]{0:T(128)S(1)}, f32[48]{0:T(128)}, u32[]{:S(2)}) copy-start(f32[48]{0:T(128)} %get-tuple-element.1249) | copy-start | bytes 580
  1130.0 218.0 %copy-start.84 = (bf16[48]{0:T(256)(128)(2,1)S(1)}, bf16[48]{0:T(256)(128)(2,1)}, u32[]{:S(2)}) copy-start(bf16[48]{0:T(256)(128)(2,1)} %copy-done.83) | copy-start | bytes 292
  1130.0 218.0 %copy-start.49 = (bf16[512,48]{1,0:T(8,128)(2,1)S(1)}, bf16[512,48]{1,0:T(8,128)(2,1)}, u32[]{:S(2)}) copy-start(bf16[512,48]{1,0:T(8,128)(2,1)} %copy-done.48) | copy-start | bytes 147460
  1130.0 489.6 %all-reduce.27.cloned.1.call-start = ((), (), s32[]{:S(2)}) async-start(), calls=%async_computation.10 | async-start | bytes 14622720 | tf_op jit(solution)/shard_map/psum | solution.py:306
  1345.7 22.4 %slice-start.2 = ((s8[6291456]{0:T(1024)(128)(4,1)}), s8[2097152]{0:T(1024)(128)(4,1)S(1)}, s32[]{:S(2)}) async-start(s8[6291456]{0:T(1024)(128)(4,1)} %bitcast.481), calls=%async_computation.13 | async-start | bytes 4194304
  1368.1 59.8 %copy-start.75 = (bf16[3072]{0:T(1024)(128)(2,1)S(1)}, bf16[3072]{0:T(1024)(128)(2,1)}, u32[]{:S(2)}) copy-start(bf16[3072]{0:T(1024)(128)(2,1)} %get-tuple-element.1095) | copy-start | bytes 18436
  (66 other events, 663.9 us)
Sparse Core Ops, SparseCore 0:
  9.6 128.1 all-gather.10
  416.3 98.1 all-gather.14
  516.1 62.4 all-gather.12
  617.2 99.0 all-gather.16
  1116.0 147.9 reduce-scatter.9
  1267.2 78.4 reduce-scatter.7
  1348.4 23.6 reduce-scatter.11
  1376.1 243.4 all-reduce.26
where the time goes:
time: 1660 us; the launch traced here: 1640 us
  waiting for transfers between devices  606 us (37%)
  local copies, waits for them, and re-layouts  345 us (21%)
  matrix products  310 us (19%)
  other arithmetic  174 us (10%)
  blocking collectives  135 us (8%)
  loops' own time  34.9 us (2%)
  between operations  20.9 us (1%)
    dynamic_update_slice x10, local copies, waits for them, and re-layouts, scan_ssd(): lax.scan(jax.checkpoint(block_step), initial, sliced)  142 us
    unnamed x10, waiting for transfers between devices  135 us
    psum x1, waiting for transfers between devices, on_device(): lax.psum(split_sums[0].astype(jnp.bfloat16), 'ctx').astype(jnp.float32)  134 us
    dot_general x6, matrix products, block_step(): y_diag = jnp.einsum('hts,shp->thp', mixing, xblock, precision=precise)  100 us
    all_gather x1, waiting for transfers between devices, on_device(): w_piece = lax.all_gather(in_matrix, 'fsdp', axis=0, tiled=True)  93.2 us
    reduce_scatter x1, waiting for transfers between devices, on_device(): lax.psum_scatter(d_out_matrix.astype(jnp.bfloat16), 'fsdp', scatter_dimen...  74.1 us
    all_gather x1, waiting for transfers between devices, prefix_2(): lax.all_gather(part.astype(kind), axis)  70.8 us
    all_gather x1, waiting for transfers between devices, prefix(): lax.all_gather(a.astype(kind), axis)  61.9 us
  transfers between devices with their start and end apart: 11, of which 7 were waited for; matrix products, arithmetic and copies ran while one was open for 9% of the time, Pallas kernels for 0%

commit v1 on v0

--- a/solution.py
+++ b/solution.py
@@ -305,7 +305,9 @@
     reduced = (
         lax.psum(split_sums[0].astype(jnp.bfloat16), "ctx").astype(jnp.float32),
         lax.psum(split_sums[1].astype(jnp.bfloat16), "ctx").astype(jnp.float32),
-        lax.psum(split_sums[2].astype(jnp.bfloat16), "ctx").astype(jnp.float32),
+        jnp.sum(lax.all_gather(split_sums[2].astype(jnp.bfloat16), "ctx"), axis=0).astype(
+            jnp.float32
+        ),
         lax.psum(split_sums[3].astype(jnp.bfloat16), "ctx").astype(jnp.float32),
         lax.psum(split_sums[4].astype(jnp.bfloat16), "ctx").astype(jnp.float32),
         lax.psum(split_sums[5].astype(jnp.bfloat16), "ctx").astype(jnp.float32),

time: 1660 us -> 1660 us (level)
    all_gather x0 -> x1, blocking collectives: none -> 31.3 us  [on_device(): lax.all_gather(split_sums[2].astype(jnp.bfloat16), 'ctx')]
where the time goes in v1:
time: 1660 us; the launch traced here: 1640 us
  waiting for transfers between devices  591 us (36%)
  local copies, waits for them, and re-layouts  345 us (21%)
  matrix products  310 us (19%)
  other arithmetic  174 us (10%)
  blocking collectives  151 us (9%)
  loops' own time  34.9 us (2%)
  between operations  20.9 us (1%)
    dynamic_update_slice x10, local copies, waits for them, and re-layouts, scan_ssd(): lax.scan(jax.checkpoint(block_step), initial, sliced)  142 us
    unnamed x10, waiting for transfers between devices  135 us
    psum x1, waiting for transfers between devices, on_device(): lax.psum(split_sums[0].astype(jnp.bfloat16), 'ctx').astype(jnp.float32)  119 us
    dot_general x6, matrix products, block_step(): y_diag = jnp.einsum('hts,shp->thp', mixing, xblock, precision=precise)  100 us
    all_gather x1, waiting for transfers between devices, on_device(): w_piece = lax.all_gather(in_matrix, 'fsdp', axis=0, tiled=True)  93.2 us
    reduce_scatter x1, waiting for transfers between devices, on_device(): lax.psum_scatter(d_out_matrix.astype(jnp.bfloat16), 'fsdp', scatter_dimen...  74.1 us
    all_gather x1, waiting for transfers between devices, prefix_2(): lax.all_gather(part.astype(kind), axis)  70.8 us
    all_gather x1, waiting for transfers between devices, prefix(): lax.all_gather(a.astype(kind), axis)  61.9 us
  transfers between devices with their start and end apart: 11, of which 7 were waited for; matrix products, arithmetic and copies ran while one was open for 9% of the time, Pallas kernels for 0%

profile of v1, /device:TPU:0, one launch (start us, length us, event | category | flops | bytes accessed | tf_op | source)
XLA Modules:
  0.0 1637.7 jit_solution(10622836766523377605)
XLA Ops:
  25.6 8.2 all-reduce.24
  33.8 5.5 all-gather.4
  44.6 93.2 %all-gather.13.cloned.1.call-done = bf16[1536,6448]{0,1:T(8,128)(2,1)} async-done(((bf16[384,6448]{0,1:T(8,128)(2,1)}), bf16[1536,6448]{0,1:T(8,128)(2,1)}) %all-gather.13.cloned.1.call-update) | async-done | bytes 19808272 | tf_op jit(solution)/shard_map/all_gather | solution.py:177
  137.8 16.7 %convolution_convert_fusion.2 = bf16[512,6448]{1,0:T(8,128)(2,1)} fusion(bf16[1536,6448]{0,1:T(8,128)(2,1)} %all-gather.13.cloned.1.call-done, bf16[1,512,1536]{2,1,0:T(8,128)(2,1)S(1)} %copy-done.14, f32[1536]{0:T(1024)S(1)} %reshape.554, f32[512]{0:T(512)S(1)} %add_rsqrt_fusion), kind=kOutput, calls=%fused_computation.150 | convolution fusion | flops 10148274176 | bytes 27992064 | tf_op jit(solution)/shard_map/dot_general | solution.py:181
  167.6 8.4 fusion.93
  175.9 6.1 slice.212
  183.9 6.6 copy.271
  190.5 8.2 reshape.509
  198.7 6.3 copy.274
  205.0 210.1 %while.80 = (s32[]{:T(128)}, f32[48,64,128]{2,1,0:T(8,128)S(1)}, s32[]{:T(128)}, f32[48]{0:T(128)S(1)}, f32[2,256,48,64]{1,0,3,2:T(2,128)}, /*index=5*/f32[2,256...) while((s32[]{:T(128)}, f32[48,64,128]{2,1,0:T(8,128)S(1)}, ...), condition=%wide.region_4.5_spmd.clone, body=%wide.region_1.4_spmd.clone.sunk | while | flops 4951254016 | bytes 38503760 | solution.py:119
  208.6 16.5 %fusion.240 = f32[48,64,256]{2,1,0:T(8,128)} fusion(f32[48,256]{1,0:T(8,128)S(1)} %dynamic-slice_bitcast_fusion.17, f32[256,256]{1,0:T(8,128)S(1)} %fusion.238, f32[48,256]{1,0:T(8,128)S(1)} %get-tuple-element.1555, pred[256,256]{1,0:T(8,128)(4,1)S(1)} %fusion.239, f32[2,256,48,64]{1,3,2,0:T(8,128)} %get-tuple-element.1662, s32[]{:T(128)} %get-tuple-element.1633), kind=kOutput, calls=%fused_computation.6.clone.1 | convolution fusion | flops 2428502016 | bytes 6767104 | tf_op jit(solution)/shard_map/jvp()/while/body/eval_jaxpr/hts,shp->thp/dot_general | solution.py:82
  236.9 63.6 %dynamic_update_slice.95 = f32[2,256,48,64]{1,0,3,2:T(2,128)} dynamic-update-slice(f32[2,256,48,64]{1,0,3,2:T(2,128)} %get-tuple-element.1637, f32[1,256,48,64]{1,0,3,2:T(1,128)} %copy.397, s32[]{:T(128)} %get-tuple-element.1633, s32[]{:T(128)} %constant.199.clone.1..sunk.1, s32[]{:T(128)} %constant.199.clone.1..sunk.1, s32[]{:T(128)} %constant.199.clone.1..sunk.1) | dynamic-update-slice | bytes 6291460 | tf_op jit(solution)/shard_map/jvp()/while/body/jit(dynamic_update_index_in_dim)/dynamic_update_slice | solution.py:119
  313.4 16.5 %fusion.240 = f32[48,64,256]{2,1,0:T(8,128)} fusion(f32[48,256]{1,0:T(8,128)S(1)} %dynamic-slice_bitcast_fusion.17, f32[256,256]{1,0:T(8,128)S(1)} %fusion.238, f32[48,256]{1,0:T(8,128)S(1)} %get-tuple-element.1555, pred[256,256]{1,0:T(8,128)(4,1)S(1)} %fusion.239, f32[2,256,48,64]{1,3,2,0:T(8,128)} %get-tuple-element.1662, s32[]{:T(128)} %get-tuple-element.1633), kind=kOutput, calls=%fused_computation.6.clone.1 | convolution fusion | flops 2428502016 | bytes 6767104 | tf_op jit(solution)/shard_map/jvp()/while/body/eval_jaxpr/hts,shp->thp/dot_general | solution.py:82
  341.7 63.6 %dynamic_update_slice.95 = f32[2,256,48,64]{1,0,3,2:T(2,128)} dynamic-update-slice(f32[2,256,48,64]{1,0,3,2:T(2,128)} %get-tuple-element.1637, f32[1,256,48,64]{1,0,3,2:T(1,128)} %copy.397, s32[]{:T(128)} %get-tuple-element.1633, s32[]{:T(128)} %constant.199.clone.1..sunk.1, s32[]{:T(128)} %constant.199.clone.1..sunk.1, s32[]{:T(128)} %constant.199.clone.1..sunk.1) | dynamic-update-slice | bytes 6291460 | tf_op jit(solution)/shard_map/jvp()/while/body/jit(dynamic_update_index_in_dim)/dynamic_update_slice | solution.py:119
  425.2 18.4 %all-gather.5 = bf16[8,1,48]{2,1,0:T(2,128)(2,1)S(1)} all-gather(bf16[1,1,48]{2,1,0:T(2,128)(2,1)S(1)} %bitcast.514), channel_id=1, replica_groups=mesh['fsdp'=4,'ctx'=8] {'ctx'}, dimensions={0}, use_global_device_ids=true | all-gather | bytes 864 | tf_op jit(solution)/shard_map/all_gather | solution.py:27
  443.6 9.0 reshape.512
  452.6 61.9 %all-gather.17.cloned.1.call-done = bf16[384,64,128]{2,1,0:T(8,128)(2,1)} async-done(((bf16[48,64,128]{2,1,0:T(8,128)(2,1)}), bf16[384,64,128]{2,1,0:T(8,128)(2,1)}) %all-gather.17.cloned.1.call-update) | async-done | bytes 6291472 | tf_op jit(solution)/shard_map/all_gather | solution.py:27
  514.7 13.1 multiply_add_fusion.4
  527.8 6.6 copy.278
  534.4 6.8 multiply_reduce_fusion.13
  541.2 37.4 %all-gather.15.cloned.1.call-done = bf16[3072,1536]{1,0:T(8,128)(2,1)} async-done(((bf16[768,1536]{1,0:T(8,128)(2,1)}), bf16[3072,1536]{1,0:T(8,128)(2,1)}) %all-gather.15.cloned.1.call-update) | async-done | bytes 9437200 | tf_op jit(solution)/shard_map/all_gather | solution.py:188
  578.6 12.5 multiply_reduce_fusion.9
  591.1 11.2 multiply_reduce_fusion.10
  602.3 6.5 copy.280
  608.8 8.2 fusion.126
  617.9 10.2 reshape.585
  628.0 11.0 copy.286
  639.0 6.4 multiply_reduce_fusion.11
  645.4 70.8 %all-gather.19.cloned.1.call-done = bf16[384,64,128]{2,1,0:T(8,128)(2,1)} async-done(((bf16[48,64,128]{2,1,0:T(8,128)(2,1)}), bf16[384,64,128]{2,1,0:T(8,128)(2,1)}) %all-gather.19.cloned.1.call-update) | async-done | bytes 6291472 | tf_op jit(solution)/shard_map/all_gather | solution.py:47
  716.2 24.0 %while.81 = (s32[]{:T(128)}, f32[48,64,128]{2,1,0:T(8,128)}, s32[]{:T(128)}, bf16[8,48]{1,0:T(8,128)(2,1)S(1)}, bf16[8,48,64,128]{3,2,1,0:T(8,128)(2,1)}, /*index=5*/s32[]{:T(128)}, s32[]{:T(128)}, s32[]{:T(128)}, s32[]{:T(128)}) while((s32[]{:T(128)}, f32[48,64,128]{2,1,0:T(8,128)}, s32[]{:T(128)}, ...), condition=%wide.region_10.11_spmd.clone, body=%wide.region_9.10_spmd.clone.sunk | while | flops 1966136 | bytes 3932807 | solution.py:63
  749.2 248.0 %while.82 = (s32[]{:T(128)}, f32[48,64,128]{2,1,0:T(8,128)}, f32[48]{0:T(128)}, f32[2,256,48,64]{1,3,2,0:T(8,128)}, f32[2,256,128]{2,1,0:T(8,128)}, /*index=5*/f...) while((s32[]{:T(128)}, f32[48,64,128]{2,1,0:T(8,128)}, ...), condition=%wide.region_26.27_spmd.clone, body=%wide.region_13.26_spmd.clone.sunk | while | flops 11239392256 | bytes 115198616 | solution.py:119
  769.1 5.3 dynamic-slice_bitcast_fusion.19
  785.5 6.7 multiply_reduce_fusion.21
  809.2 21.4 %fusion.264 = (f32[48,256]{1,0:T(8,128)S(1)}, f32[48,256]{1,0:T(8,128)S(1)}, f32[48,256]{1,0:T(8,128)}, f32[256,256]{1,0:T(8,128)}) fusion(f32[48,256]{1,0:T(8,128)S(1)} %bitcast.485, f32[256,256]{1,0:T(8,128)S(1)} %fusion.262, f32[48,256]{1,0:T(8,128)} %get-tuple-element.1593, pred[256,256]{1,0:T(8,128)(4,1)S(1)} %fusion.263, ...), kind=kOutput, calls=%fused_computation.72.clone.1 | convolution fusion | flops 2456711168 | bytes 7127040 | tf_op jit(solution)/shard_map/transpose(jvp())/while/body/eval_jaxpr/checkpoint/hts,shp->thp/dot_general | solution.py:82
  844.3 6.4 fusion.269
  852.8 6.5 fusion.267
  860.7 12.2 bitcast_dynamic-update-slice_fusion.7
  878.7 5.3 dynamic-slice_bitcast_fusion.19
  895.7 6.7 multiply_reduce_fusion.21
  919.4 21.4 %fusion.264 = (f32[48,256]{1,0:T(8,128)S(1)}, f32[48,256]{1,0:T(8,128)S(1)}, f32[48,256]{1,0:T(8,128)}, f32[256,256]{1,0:T(8,128)}) fusion(f32[48,256]{1,0:T(8,128)S(1)} %bitcast.485, f32[256,256]{1,0:T(8,128)S(1)} %fusion.262, f32[48,256]{1,0:T(8,128)} %get-tuple-element.1593, pred[256,256]{1,0:T(8,128)(4,1)S(1)} %fusion.263, ...), kind=kOutput, calls=%fused_computation.72.clone.1 | convolution fusion | flops 2456711168 | bytes 7127040 | tf_op jit(solution)/shard_map/transpose(jvp())/while/body/eval_jaxpr/checkpoint/hts,shp->thp/dot_general | solution.py:82
  954.6 6.4 fusion.269
  963.0 6.5 fusion.267
  971.0 12.2 bitcast_dynamic-update-slice_fusion.7
  997.2 12.7 fusion.132
  1009.9 11.3 copy.299
  1021.2 10.8 reshape.586
  1032.0 6.0 multiply_add_fusion.3
  1038.1 10.7 multiply_reduce_fusion.8
  1048.8 8.2 broadcast_multiply_fusion
  1057.0 8.0 fusion.165
  1075.3 16.4 convolution_convert_fusion
  1091.6 24.2 %copy.300 = bf16[1536,6448]{1,0:T(8,128)(2,1)} copy(bf16[1536,6448]{0,1:T(8,128)(2,1)} %convolution_convert_fusion) | data formatting | bytes 39616512
  1117.2 11.2 convolution_convert_fusion.1
  1130.3 133.6 %reduce-scatter.10.cloned.1.call-done = bf16[384,6448]{1,0:T(8,128)(2,1)} async-done(((bf16[1536,6448]{1,0:T(8,128)(2,1)}), bf16[384,6448]{1,0:T(8,128)(2,1)}) %reduce-scatter.10.cloned.1.call-update) | async-done | bytes 4952080
  1264.0 7.6 copy.301
  1271.5 74.1 %reduce-scatter.8.cloned.1.call-done = bf16[768,1536]{1,0:T(8,128)(2,1)} async-done(((bf16[3072,1536]{1,0:T(8,128)(2,1)}), bf16[768,1536]{1,0:T(8,128)(2,1)}) %reduce-scatter.8.cloned.1.call-update) | async-done | bytes 2359312 | tf_op jit(solution)/shard_map/reduce_scatter | solution.py:289
  1348.0 20.0 %fusion.135 = f32[512,1536]{1,0:T(8,128)S(1)} fusion(bf16[1536,6448]{0,1:T(8,128)(2,1)} %all-gather.13.cloned.1.call-done, bf16[512,48]{1,0:T(8,128)(2,1)S(1)} %copy-done.49, bf16[3,3328]{1,0:T(4,128)(2,1)S(1)} %fusion.147, bf16[509,3328]{1,0:T(8,128)(2,1)} %copy-done.19, bf16[512,3072]{1,0:T(8,128)(2,1)} %get-tuple-element.1247), kind=kOutput, calls=%fused_computation.222 | convolution fusion | flops 10168238080 | bytes 29556736 | tf_op jit(solution)/shard_map/dot_general | solution.py:275
  1368.1 12.7 multiply_reduce_fusion.15
  1382.2 44.0 %all-reduce.20 = (f32[48]{0:T(128)S(1)}, f32[48]{0:T(128)S(1)}, f32[48]{0:T(128)S(1)}, f32[2]{0:T(128)S(1)}) all-reduce(f32[48]{0:T(128)S(1)} %copy-done.80, f32[48]{0:T(128)S(1)} %fusion.156, f32[48]{0:T(128)S(1)} %reduce_sum.389, f32[2]{0:T(128)S(1)} %pad_maximum_fusion.3), channel_id=1, replica_groups=mesh['fsdp'=4,'ctx'=8] {'fsdp','ctx'}, use_global_device_ids=true, to_apply=%region_42.43 | all-reduce | flops 146 | bytes 1168 | tf_op jit(solution)/shard_map/psum | solution.py:316
  1427.9 11.9 all-reduce.23
  1440.0 21.3 %all-reduce.21 = (bf16[832]{0:T(1024)(128)(2,1)S(1)}, bf16[768]{0:T(1024)(128)(2,1)S(1)}, bf16[384]{0:T(512)(128)(2,1)S(1)}) all-reduce(bf16[832]{0:T(1024)(128)(2,1)S(1)} %dynamic-slice.5, bf16[768]{0:T(1024)(128)(2,1)S(1)} %dynamic-slice.7, bf16[384]{0:T(512)(128)(2,1)S(1)} %dynamic-slice.9), channel_id=1, replica_groups=mesh['fsdp'=4,'ctx'=8] {'ctx'}, use_global_device_ids=true, to_apply=%region_40.41 | all-reduce | flops 1984 | bytes 7936 | tf_op jit(solution)/shard_map/psum | solution.py:311
  1469.6 31.3 %all-gather.7 = bf16[8,832,4]{1,2,0:T(4,128)(2,1)S(1)} all-gather(bf16[1,832,4]{1,2,0:T(4,128)(2,1)S(1)} %bitcast.509), channel_id=4, replica_groups=mesh['fsdp'=4,'ctx'=8] {'ctx'}, dimensions={0}, use_global_device_ids=true | all-gather | bytes 59904 | tf_op jit(solution)/shard_map/all_gather | solution.py:308
  1501.5 119.0 %all-reduce.27.cloned.1.call-done = (bf16[384,6448]{0,1:T(8,128)(2,1)}, bf16[768,1536]{1,0:T(8,128)(2,1)}) async-done(((bf16[384,6448]{0,1:T(8,128)(2,1)}, bf16[768,1536]{1,0:T(8,128)(2,1)}), (bf16[384,6448]{0,1:T(8,128)(2,1)}, bf16[768,1536]{1,0:T(8,128)(2,1)})) %all-reduce.27.cloned.1.call-update) | async-done | bytes 7311376 | tf_op jit(solution)/shard_map/psum | solution.py:306
  1620.5 7.1 convert_element_type.265
  (497 shorter events, 253.8 us)
Async XLA Ops:
  7.2 36.1 %copy-start.68 = (s32[1,512]{1,0:T(1,128)S(1)}, s32[1,512]{1,0:T(1,128)}, u32[]{:S(2)}) copy-start(s32[1,512]{1,0:T(1,128)} %param.21) | copy-start | bytes 6148
  7.2 34.3 %copy-start.14 = (bf16[1,512,1536]{2,1,0:T(8,128)(2,1)S(1)}, bf16[1,512,1536]{2,1,0:T(8,128)(2,1)}, u32[]{:S(2)}) copy-start(bf16[1,512,1536]{2,1,0:T(8,128)(2,1)} %param.20) | copy-start | bytes 4718596
  7.2 130.6 %all-gather.13.cloned.1.call-start = ((), (), s32[]{:S(2)}) async-start(), calls=%async_computation.3 | async-start | bytes 24760320 | tf_op jit(solution)/shard_map/all_gather | solution.py:177
  7.9 506.6 %all-gather.17.cloned.1.call-start = ((), (), s32[]{:S(2)}) async-start(), calls=%async_computation.6 | async-start | bytes 7077888 | tf_op jit(solution)/shard_map/all_gather | solution.py:27
  8.7 33.3 %collective-permute-start = (s32[3]{0:T(128)S(1)}, s32[3]{0:T(128)S(1)}, u32[]{:S(2)}, u32[]{:S(2)}) collective-permute-start(s32[3]{0:T(128)S(1)} %slice_bitcast_fusion), channel_id=1, source_target_pairs={{0,1},{1,2},{2,3},{3,4},{4,5},{5,6},{6,7},{8,9},{9,10},{10,11},{11... | collective-permute-start | bytes 44 | tf_op jit(solution)/shard_map/ppermute | solution.py:21
  19.5 135.0 %copy-start.65 = (f32[1536]{0:T(1024)}, f32[1536]{0:T(1024)S(1)}, u32[]{:S(2)}) copy-start(f32[1536]{0:T(1024)S(1)} %reshape.554) | copy-start | bytes 18436
  33.8 120.7 %copy-start.83 = (bf16[48]{0:T(256)(128)(2,1)}, bf16[48]{0:T(256)(128)(2,1)S(1)}, u32[]{:S(2)}) copy-start(bf16[48]{0:T(256)(128)(2,1)S(1)} %get-tuple-element.1205) | copy-start | bytes 292
  39.5 119.4 %copy-start.76 = (f32[48]{0:T(128)}, f32[48]{0:T(128)S(1)}, u32[]{:S(2)}) copy-start(f32[48]{0:T(128)S(1)} %convert_element_type.243) | copy-start | bytes 580
  41.5 126.0 %copy-start.40 = (f32[3328]{0:T(1024)}, f32[3328]{0:T(1024)S(1)}, u32[]{:S(2)}) copy-start(f32[3328]{0:T(1024)S(1)} %get-tuple-element.1104) | copy-start | bytes 39940
  41.5 126.0 %copy-start.42 = (f32[3328]{0:T(1024)}, f32[3328]{0:T(1024)S(1)}, u32[]{:S(2)}) copy-start(f32[3328]{0:T(1024)S(1)} %get-tuple-element.1105) | copy-start | bytes 39940
  41.6 126.0 %copy-start.44 = (f32[3328]{0:T(1024)}, f32[3328]{0:T(1024)S(1)}, u32[]{:S(2)}) copy-start(f32[3328]{0:T(1024)S(1)} %get-tuple-element.1106) | copy-start | bytes 39940
  41.6 126.0 %copy-start.46 = (f32[3328]{0:T(1024)}, f32[3328]{0:T(1024)S(1)}, u32[]{:S(2)}) copy-start(f32[3328]{0:T(1024)S(1)} %get-tuple-element.1107) | copy-start | bytes 39940
  42.0 117.0 %copy-start.78 = (f32[48]{0:T(128)}, f32[48]{0:T(128)S(1)}, u32[]{:S(2)}) copy-start(f32[48]{0:T(128)S(1)} %convert_exponential_fusion) | copy-start | bytes 580
  42.0 112.5 %copy-start.73 = (f32[512]{0:T(512)}, f32[512]{0:T(512)S(1)}, u32[]{:S(2)}) copy-start(f32[512]{0:T(512)S(1)} %add_rsqrt_fusion) | copy-start | bytes 6148
  44.6 123.0 %copy-start.59 = (f32[512]{0:T(512)}, f32[512]{0:T(512)S(1)}, u32[]{:S(2)}) copy-start(f32[512]{0:T(512)S(1)} %get-tuple-element.1258) | copy-start | bytes 6148
  44.6 123.0 %copy-start.61 = (f32[512]{0:T(512)}, f32[512]{0:T(512)S(1)}, u32[]{:S(2)}) copy-start(f32[512]{0:T(512)S(1)} %get-tuple-element.1259) | copy-start | bytes 6148
  44.6 123.0 %copy-start.63 = (f32[512]{0:T(512)}, f32[512]{0:T(512)S(1)}, u32[]{:S(2)}) copy-start(f32[512]{0:T(512)S(1)} %get-tuple-element.1260) | copy-start | bytes 6148
  155.3 9.5 collective-permute-start.1
  205.0 212.5 %copy-start.81 = (bf16[768]{0:T(1024)(128)(2,1)S(1)}, bf16[768]{0:T(1024)(128)(2,1)}, u32[]{:S(2)}) copy-start(bf16[768]{0:T(1024)(128)(2,1)} %param.30) | copy-start | bytes 4612
  415.1 37.5 %copy-start.50 = (s32[2,256]{1,0:T(2,128)}, s32[2,256]{1,0:T(2,128)S(1)}, u32[]{:S(2)}) copy-start(s32[2,256]{1,0:T(2,128)S(1)} %get-tuple-element.1821) | copy-start | bytes 6148
  416.2 162.4 %all-gather.15.cloned.1.call-start = ((), (), s32[]{:S(2)}) async-start(), calls=%async_computation.4 | async-start | bytes 11796480 | tf_op jit(solution)/shard_map/all_gather | solution.py:188
  416.9 299.3 %all-gather.19.cloned.1.call-start = ((), (), s32[]{:S(2)}) async-start(), calls=%async_computation.7 | async-start | bytes 7077888 | tf_op jit(solution)/shard_map/all_gather | solution.py:47
  422.7 168.4 %copy-start.55 = (f32[4,1,768]{2,1,0:T(1,128)}, f32[4,1,768]{2,1,0:T(1,128)S(1)}, u32[]{:S(2)}) copy-start(f32[4,1,768]{2,1,0:T(1,128)S(1)} %convert_element_type.283) | copy-start | bytes 36868
  452.6 156.2 %copy-start.24 = (f32[512,48]{0,1:T(8,128)}, f32[512,48]{0,1:T(8,128)S(1)}, u32[]{:S(2)}) copy-start(f32[512,48]{0,1:T(8,128)S(1)} %exponential_multiply_fusion.4) | copy-start | bytes 294916
  514.7 225.5 %copy-start.2 = (f32[48,64,128]{2,1,0:T(8,128)}, f32[48,64,128]{2,1,0:T(8,128)S(1)}, u32[]{:S(2)}) copy-start(f32[48,64,128]{2,1,0:T(8,128)S(1)} %get-tuple-element.688) | copy-start | bytes 4718596
  534.4 44.2 %copy-start.27 = (bf16[1,512,1536]{2,1,0:T(8,128)(2,1)S(1)}, bf16[1,512,1536]{2,1,0:T(8,128)(2,1)}, u32[]{:S(2)}) copy-start(bf16[1,512,1536]{2,1,0:T(8,128)(2,1)} %param.22) | copy-start | bytes 4718596
  541.2 49.9 %copy-start.71 = (f32[512]{0:T(512)}, f32[512]{0:T(512)S(1)}, u32[]{:S(2)}) copy-start(f32[512]{0:T(512)S(1)} %fusion.153) | copy-start | bytes 6148
  617.1 646.9 %reduce-scatter.10.cloned.1.call-start = ((), (), s32[]{:S(2)}) async-start(), calls=%async_computation.8 | async-start | bytes 25067520
  776.8 32.3 %copy-start.8 = (f32[256,48]{0,1:T(8,128)}, f32[256,48]{0,1:T(8,128)S(1)}, u32[]{:S(2)}) copy-start(f32[256,48]{0,1:T(8,128)S(1)} %get-tuple-element.1589) | copy-start | bytes 147460 | tf_op jit(solution)/shard_map/transpose(jvp())/while
  808.3 22.4 %copy-start.12 = (f32[256,256]{1,0:T(8,128)}, f32[256,256]{1,0:T(8,128)S(1)}, u32[]{:S(2)}) copy-start(f32[256,256]{1,0:T(8,128)S(1)} %fusion.262) | copy-start | bytes 786436 | tf_op jit(solution)/shard_map/transpose(jvp())/while
  809.1 21.5 %copy-start.25 = (pred[256,256]{1,0:T(8,128)(4,1)}, pred[256,256]{1,0:T(8,128)(4,1)S(1)}, u32[]{:S(2)}) copy-start(pred[256,256]{1,0:T(8,128)(4,1)S(1)} %fusion.263) | copy-start | bytes 196612 | tf_op jit(solution)/shard_map/transpose(jvp())/while
  809.1 21.5 %copy-start.18 = (f32[1,256,48]{1,2,0:T(8,128)S(1)}, f32[1,256,48]{1,2,0:T(8,128)}, u32[]{:S(2)}) copy-start(f32[1,256,48]{1,2,0:T(8,128)} %copy.405) | copy-start | bytes 147460 | tf_op jit(solution)/shard_map/transpose(jvp())/while
  809.2 21.5 %copy-start.22 = (f32[1,48]{0,1:T(8,128)S(1)}, f32[1,48]{0,1:T(8,128)}, u32[]{:S(2)}) copy-start(f32[1,48]{0,1:T(8,128)} %copy.406) | copy-start | bytes 580 | tf_op jit(solution)/shard_map/transpose(jvp())/while
  809.2 21.5 %copy-start.35 = (f32[48,2]{0,1:T(2,128)S(1)}, f32[48,2]{0,1:T(2,128)}, u32[]{:S(2)}) copy-start(f32[48,2]{0,1:T(2,128)} %copy-done.34) | copy-start | bytes 1156 | tf_op jit(solution)/shard_map/transpose(jvp())/while
  809.2 21.5 %copy-start.36 = (f32[256]{0:T(256)S(1)}, f32[256]{0:T(256)}, u32[]{:S(2)}) copy-start(f32[256]{0:T(256)} %get-tuple-element.1601) | copy-start | bytes 3076 | tf_op jit(solution)/shard_map/transpose(jvp())/while
  809.2 21.5 %copy-start.39 = (f32[48]{0:T(128)S(1)}, f32[48]{0:T(128)}, u32[]{:S(2)}) copy-start(f32[48]{0:T(128)} %copy-done.38) | copy-start | bytes 580 | tf_op jit(solution)/shard_map/transpose(jvp())/while
  809.2 21.5 %copy-start.52 = (f32[256]{0:T(256)S(1)}, f32[256]{0:T(256)}, u32[]{:S(2)}) copy-start(f32[256]{0:T(256)} %get-tuple-element.1606) | copy-start | bytes 3076 | tf_op jit(solution)/shard_map/transpose(jvp())/while
  840.0 20.6 %copy-start.3 = (f32[256,48,64]{0,2,1:T(8,128)S(1)}, f32[256,48,64]{0,2,1:T(8,128)}, u32[]{:S(2)}) copy-start(f32[256,48,64]{0,2,1:T(8,128)} %get-tuple-element.1610) | copy-start | bytes 9437188 | tf_op jit(solution)/shard_map/transpose(jvp())/while
  840.0 20.6 %copy-start.9 = (f32[256,48]{0,1:T(8,128)S(1)}, f32[256,48]{0,1:T(8,128)}, u32[]{:S(2)}) copy-start(f32[256,48]{0,1:T(8,128)} %copy-done.8) | copy-start | bytes 147460 | tf_op jit(solution)/shard_map/transpose(jvp())/while
  840.0 20.6 %copy-start.13 = (f32[256,256]{1,0:T(8,128)S(1)}, f32[256,256]{1,0:T(8,128)}, u32[]{:S(2)}) copy-start(f32[256,256]{1,0:T(8,128)} %copy-done.12) | copy-start | bytes 786436 | tf_op jit(solution)/shard_map/transpose(jvp())/while
  886.4 33.0 %copy-start.8 = (f32[256,48]{0,1:T(8,128)}, f32[256,48]{0,1:T(8,128)S(1)}, u32[]{:S(2)}) copy-start(f32[256,48]{0,1:T(8,128)S(1)} %get-tuple-element.1589) | copy-start | bytes 147460 | tf_op jit(solution)/shard_map/transpose(jvp())/while
  918.5 22.4 %copy-start.12 = (f32[256,256]{1,0:T(8,128)}, f32[256,256]{1,0:T(8,128)S(1)}, u32[]{:S(2)}) copy-start(f32[256,256]{1,0:T(8,128)S(1)} %fusion.262) | copy-start | bytes 786436 | tf_op jit(solution)/shard_map/transpose(jvp())/while
  919.4 21.5 %copy-start.25 = (pred[256,256]{1,0:T(8,128)(4,1)}, pred[256,256]{1,0:T(8,128)(4,1)S(1)}, u32[]{:S(2)}) copy-start(pred[256,256]{1,0:T(8,128)(4,1)S(1)} %fusion.263) | copy-start | bytes 196612 | tf_op jit(solution)/shard_map/transpose(jvp())/while
  919.4 21.5 %copy-start.18 = (f32[1,256,48]{1,2,0:T(8,128)S(1)}, f32[1,256,48]{1,2,0:T(8,128)}, u32[]{:S(2)}) copy-start(f32[1,256,48]{1,2,0:T(8,128)} %copy.405) | copy-start | bytes 147460 | tf_op jit(solution)/shard_map/transpose(jvp())/while
  919.4 21.5 %copy-start.22 = (f32[1,48]{0,1:T(8,128)S(1)}, f32[1,48]{0,1:T(8,128)}, u32[]{:S(2)}) copy-start(f32[1,48]{0,1:T(8,128)} %copy.406) | copy-start | bytes 580 | tf_op jit(solution)/shard_map/transpose(jvp())/while
  919.4 21.5 %copy-start.35 = (f32[48,2]{0,1:T(2,128)S(1)}, f32[48,2]{0,1:T(2,128)}, u32[]{:S(2)}) copy-start(f32[48,2]{0,1:T(2,128)} %copy-done.34) | copy-start | bytes 1156 | tf_op jit(solution)/shard_map/transpose(jvp())/while
  919.4 21.5 %copy-start.36 = (f32[256]{0:T(256)S(1)}, f32[256]{0:T(256)}, u32[]{:S(2)}) copy-start(f32[256]{0:T(256)} %get-tuple-element.1601) | copy-start | bytes 3076 | tf_op jit(solution)/shard_map/transpose(jvp())/while
  919.4 21.5 %copy-start.39 = (f32[48]{0:T(128)S(1)}, f32[48]{0:T(128)}, u32[]{:S(2)}) copy-start(f32[48]{0:T(128)} %copy-done.38) | copy-start | bytes 580 | tf_op jit(solution)/shard_map/transpose(jvp())/while
  919.4 21.5 %copy-start.52 = (f32[256]{0:T(256)S(1)}, f32[256]{0:T(256)}, u32[]{:S(2)}) copy-start(f32[256]{0:T(256)} %get-tuple-element.1606) | copy-start | bytes 3076 | tf_op jit(solution)/shard_map/transpose(jvp())/while
  950.3 20.7 %copy-start.3 = (f32[256,48,64]{0,2,1:T(8,128)S(1)}, f32[256,48,64]{0,2,1:T(8,128)}, u32[]{:S(2)}) copy-start(f32[256,48,64]{0,2,1:T(8,128)} %get-tuple-element.1610) | copy-start | bytes 9437188 | tf_op jit(solution)/shard_map/transpose(jvp())/while
  950.3 20.7 %copy-start.9 = (f32[256,48]{0,1:T(8,128)S(1)}, f32[256,48]{0,1:T(8,128)}, u32[]{:S(2)}) copy-start(f32[256,48]{0,1:T(8,128)} %copy-done.8) | copy-start | bytes 147460 | tf_op jit(solution)/shard_map/transpose(jvp())/while
  950.3 20.6 %copy-start.13 = (f32[256,256]{1,0:T(8,128)S(1)}, f32[256,256]{1,0:T(8,128)}, u32[]{:S(2)}) copy-start(f32[256,256]{1,0:T(8,128)} %copy-done.12) | copy-start | bytes 786436 | tf_op jit(solution)/shard_map/transpose(jvp())/while
  950.3 20.6 %copy-start.17 = (f32[256,48]{0,1:T(8,128)S(1)}, f32[256,48]{0,1:T(8,128)}, u32[]{:S(2)}) copy-start(f32[256,48]{0,1:T(8,128)} %get-tuple-element.1611) | copy-start | bytes 147460 | tf_op jit(solution)/shard_map/transpose(jvp())/while
  950.3 20.6 %copy-start.26 = (pred[256,256]{1,0:T(8,128)(4,1)S(1)}, pred[256,256]{1,0:T(8,128)(4,1)}, u32[]{:S(2)}) copy-start(pred[256,256]{1,0:T(8,128)(4,1)} %copy-done.25) | copy-start | bytes 196612 | tf_op jit(solution)/shard_map/transpose(jvp())/while
  1065.7 7.9 collective-permute-start.2
  1115.9 229.8 %reduce-scatter.8.cloned.1.call-start = ((), (), s32[]{:S(2)}) async-start(), calls=%async_computation.5 | async-start | bytes 11796480 | tf_op jit(solution)/shard_map/reduce_scatter | solution.py:289
  1128.5 340.1 %reduce-scatter.12.cloned.1.call-start = ((), (), s32[]{:S(2)}) async-start(), calls=%async_computation.9 | async-start | bytes 1064960
  1130.0 217.8 %copy-start.57 = (f32[3072]{0:T(1024)S(1)}, f32[3072]{0:T(1024)}, u32[]{:S(2)}) copy-start(f32[3072]{0:T(1024)} %get-tuple-element.1210) | copy-start | bytes 36868
  1130.0 218.0 %copy-start.82 = (f32[48]{0:T(128)S(1)}, f32[48]{0:T(128)}, u32[]{:S(2)}) copy-start(f32[48]{0:T(128)} %get-tuple-element.1248) | copy-start | bytes 580
  1130.0 218.0 %copy-start.84 = (bf16[48]{0:T(256)(128)(2,1)S(1)}, bf16[48]{0:T(256)(128)(2,1)}, u32[]{:S(2)}) copy-start(bf16[48]{0:T(256)(128)(2,1)} %copy-done.83) | copy-start | bytes 292
  1130.0 218.0 %copy-start.49 = (bf16[512,48]{1,0:T(8,128)(2,1)S(1)}, bf16[512,48]{1,0:T(8,128)(2,1)}, u32[]{:S(2)}) copy-start(bf16[512,48]{1,0:T(8,128)(2,1)} %copy-done.48) | copy-start | bytes 147460
  1130.0 490.5 %all-reduce.27.cloned.1.call-start = ((), (), s32[]{:S(2)}) async-start(), calls=%async_computation.10 | async-start | bytes 14622720 | tf_op jit(solution)/shard_map/psum | solution.py:306
  1345.7 22.4 %slice-start.2 = ((s8[6291456]{0:T(1024)(128)(4,1)}), s8[2097152]{0:T(1024)(128)(4,1)S(1)}, s32[]{:S(2)}) async-start(s8[6291456]{0:T(1024)(128)(4,1)} %bitcast.482), calls=%async_computation.13 | async-start | bytes 4194304
  1368.1 59.8 %copy-start.75 = (bf16[3072]{0:T(1024)(128)(2,1)S(1)}, bf16[3072]{0:T(1024)(128)(2,1)}, u32[]{:S(2)}) copy-start(bf16[3072]{0:T(1024)(128)(2,1)} %get-tuple-element.1095) | copy-start | bytes 18436
  (66 other events, 663.9 us)
Sparse Core Ops, SparseCore 0:
  9.6 128.1 all-gather.12
  416.3 98.1 all-gather.16
  516.1 62.4 all-gather.14
  617.2 99.0 all-gather.18
  1116.0 147.9 reduce-scatter.9
  1267.2 78.4 reduce-scatter.7
  1348.4 23.6 reduce-scatter.11
  1376.1 244.3 all-reduce.26
